TPU v7x, 32 devices: a whole 2x2x4 slice. The times are simulated.
32 devices in a mesh: dp: 8 (over z, y), row: 2 (over core), col: 2 (over x).
Axes of the slice: x: 2, y: 2, z: 4, core: 2. Of those that a mesh axis runs over, the one named last changes fastest.
Arguments:
- tokens: bfloat16 [32768, 768], P(('dp', 'col'), 'row'), may hold values from -6 to 6
- w_query: float32 [768, 768], P('row', 'col'), may hold values from -0.21875 to 0.21875
- w_key: float32 [768, 768], P('row', 'col'), may hold values from -0.21875 to 0.21875
- w_value: float32 [768, 768], P('row', 'col'), may hold values from -0.21875 to 0.21875
- w_attn_out: float32 [768, 768], P('col', 'row'), may hold values from -0.875 to 0.875
- w_inter: float32 [768, 3072], P('row', 'col'), may hold values from -0.21875 to 0.21875
- w_ffout: float32 [3072, 768], P('col', 'row'), may hold values from -0.109375 to 0.109375
- b_query: float32 [768], replicated, may hold values from -3 to 3
- b_value: float32 [768], replicated, may hold values from -3 to 3
- b_attn_out: float32 [768], replicated, may hold values from -3 to 3
- b_inter: float32 [3072], replicated, may hold values from -3 to 3
- b_ffout: float32 [768], replicated, may hold values from -3 to 3
- gain_one: float32 [768], replicated, may hold values from 0.25 to 1.75
- shift_one: float32 [768], replicated, may hold values from -3 to 3
- gain_two: float32 [768], replicated, may hold values from 0.25 to 1.75
- shift_two: float32 [768], replicated, may hold values from -3 to 3
- lengths: int32 [16], replicated, may hold values from 1025 to 2048, as said below
- block_order: int32 [12, 2], replicated, may hold values from 0 to 1, each once within a row
- cotangent: bfloat16 [32768, 768], P(('dp', 'col'), 'row'), may hold values from -6 to 6
Outputs:
- layer_out: bfloat16 [32768, 768], P(('dp', 'col'), 'row')
- grad_tokens: float32 [32768, 768], P(('dp', 'col'), 'row')
- grad_w_query: float32 [768, 768], P('row', 'col')
- grad_w_key: float32 [768, 768], P('row', 'col')
- grad_w_value: float32 [768, 768], P('row', 'col')
- grad_w_attn_out: float32 [768, 768], P('col', 'row')
- grad_w_inter: float32 [768, 3072], P('row', 'col')
- grad_w_ffout: float32 [3072, 768], P('col', 'row')
- grad_b_query: float32 [768], replicated
- grad_b_value: float32 [768], replicated
- grad_b_attn_out: float32 [768], replicated
- grad_b_inter: float32 [3072], replicated
- grad_b_ffout: float32 [768], replicated
- grad_gain_one: float32 [768], replicated
- grad_shift_one: float32 [768], replicated
- grad_gain_two: float32 [768], replicated
- grad_shift_two: float32 [768], replicated
Inputs may be any that keep to these rules, and one draw needn't show every extreme that they name: `lengths`: every sequence is longer than half of 2048; one sequence fills all 2048 slots. `block_order`: each row holds 0 and 1 once each.
All inputs are finite; a program needn't handle non-finite values.
Results may differ from a plain program's by a relative error of at most 0.02.
Values may be sent and summed in bfloat16 or wider, within the bound.
No kernel may reach another device: no remote copies, remote signals or barrier semaphores. Data moves between devices by JAX's collectives and lax.ppermute only.
A program may use at most 192 MiB of HBM per device.

v0:
```python
import jax
import jax.numpy as jnp
from jax import lax
from jax.sharding import PartitionSpec as P

D = 768
HD = 64
FF = 3072
SEQ = 2048
eps_norm = 1e-05
masked_score = -1e30


def product(left, right):
    return jnp.dot(left, right, preferred_element_type=jnp.float32)


def transposed(left, right):
    return lax.dot_general(
        left, right, (((1,), (1,)), ((), ())), preferred_element_type=jnp.float32
    )


def outer_sum(left, right):
    return lax.dot_general(
        left, right, (((0,), (0,)), ((), ())), preferred_element_type=jnp.float32
    )


def gelu_exact(values):
    return jax.nn.gelu(values, approximate=False)


def placed(values, start, total):
    return lax.dynamic_update_slice(jnp.zeros((total,), jnp.float32), values, (start,))


def gather_cols(values):
    return lax.all_gather(values, "col", axis=0, tiled=True)


def gather_rows(values):
    return lax.all_gather(values, "row", axis=0, tiled=True)


def sum_rows(values):
    return lax.psum_scatter(values, "row", scatter_dimension=0, tiled=True)


def sum_cols(values):
    return lax.psum_scatter(
        values.astype(jnp.bfloat16), "col", scatter_dimension=0, tiled=True
    ).astype(jnp.float32)


def shared_sums(total_one, total_two):
    return lax.psum((total_one, total_two), "row")


def norm_forward(values, gain, shift, reducer):
    total, squares = reducer(jnp.sum(values, 1), jnp.sum(values * values, 1))
    mean = total / D
    variance = squares / D - mean * mean
    scale = lax.rsqrt(variance + eps_norm)
    normal = (values - mean[:, None]) * scale[:, None]
    return (normal * gain + shift, normal, scale)


def norm_backward(grad, normal, scale, gain, reducer):
    inner = grad * gain
    sum_plain, sum_normal = reducer(jnp.sum(inner, 1), jnp.sum(inner * normal, 1))
    return scale[:, None] * (inner - sum_plain[:, None] / D - normal * (sum_normal / D)[:, None])


def head_block(
    query, key_all, value_all, orders, lengths_here, index, heads_local, parts, my_part, seq_rows
):
    half = SEQ // 2
    per_seq = heads_local * parts
    seq_index = index // per_seq
    head = index % per_seq // parts
    offset = index % parts
    part = offset + my_part
    source = orders[head, part]
    query_row = seq_index * seq_rows + offset * half
    select = source * 0
    key_row = seq_index * seq_rows + source * half
    column = head * HD
    query_block = lax.dynamic_slice(query, (query_row, column), (half, HD))
    key_block = lax.dynamic_slice(key_all, (select, key_row, column), (1, half, HD))[0]
    value_block = lax.dynamic_slice(value_all, (select, key_row, column), (1, half, HD))[0]
    positions = source * half + jnp.arange(half)
    live = positions < lengths_here[seq_index]
    scores = transposed(query_block, key_block) * HD ** (-0.5)
    scores = jnp.where(live[None, :], scores, masked_score)
    return (query_row, key_row, select, column, head, query_block, key_block, value_block, scores)


def attend_forward(query, key_all, value_all, orders, lengths_here, parts, my_part, seq_rows):
    rows, width = query.shape
    heads_local = width // HD
    count = rows // seq_rows * heads_local * parts

    def step(index, carry):
        blended_attention_output, logsum = carry
        query_row, key_row, select, column, head, query_block, key_block, value_block, scores = (
            head_block(
                query,
                key_all,
                value_all,
                orders,
                lengths_here,
                index,
                heads_local,
                parts,
                my_part,
                seq_rows,
            )
        )
        top = jnp.max(scores, 1, keepdims=True)
        expo = jnp.exp(scores - top)
        total = jnp.sum(expo, 1, keepdims=True)
        attention_probabilities = (expo / total).astype(jnp.bfloat16)
        blended_attention_output = lax.dynamic_update_slice(
            blended_attention_output,
            product(attention_probabilities, value_block),
            (query_row, column),
        )
        logsum = lax.dynamic_update_slice(logsum, top + jnp.log(total), (query_row, head))
        return (blended_attention_output, logsum)

    start = (jnp.zeros((rows, width), jnp.float32), jnp.zeros((rows, heads_local), jnp.float32))
    return lax.fori_loop(0, count, step, start)


def attend_backward(
    query, key_all, value_all, grad_mixed, logsum, orders, lengths_here, parts, my_part, seq_rows
):
    rows, width = query.shape
    heads_local = width // HD
    count = rows // seq_rows * heads_local * parts
    half = SEQ // 2

    def step(index, carry):
        grad_query, grad_key, grad_value = carry
        query_row, key_row, select, column, head, query_block, key_block, value_block, scores = (
            head_block(
                query,
                key_all,
                value_all,
                orders,
                lengths_here,
                index,
                heads_local,
                parts,
                my_part,
                seq_rows,
            )
        )
        logsum_block = lax.dynamic_slice(logsum, (query_row, head), (half, 1))
        attention_probabilities = jnp.exp(scores - logsum_block)
        grad_block = lax.dynamic_slice(grad_mixed, (query_row, column), (half, HD))
        grad_probs = transposed(grad_block, value_block)
        inner = jnp.sum(grad_probs * attention_probabilities, 1, keepdims=True)
        grad_scores = (attention_probabilities * (grad_probs - inner) * HD ** (-0.5)).astype(
            jnp.bfloat16
        )
        grad_query = lax.dynamic_update_slice(
            grad_query, product(grad_scores, key_block), (query_row, column)
        )
        grad_key = lax.dynamic_update_slice(
            grad_key, outer_sum(grad_scores, query_block)[None], (select, key_row, column)
        )
        grad_value = lax.dynamic_update_slice(
            grad_value,
            outer_sum(attention_probabilities.astype(jnp.bfloat16), grad_block)[None],
            (select, key_row, column),
        )
        return (grad_query, grad_key, grad_value)

    empty_query = jnp.zeros((rows, width), jnp.float32)
    empty_keys = jnp.zeros(key_all.shape, jnp.float32)
    return lax.fori_loop(0, count, step, (empty_query, empty_keys, empty_keys))


def grid_plan(tokens, weights, vectors, lengths, block_order, cotangent):
    w_query, w_key, w_value, w_attn_out, w_inter, w_ffout = weights
    b_query, b_value, b_attn_out, b_inter, b_ffout, gain_one, shift_one, gain_two, shift_two = (
        vectors
    )
    rows_col, width_row = tokens.shape
    width_col = w_query.shape[1]
    ff_col = w_inter.shape[1]
    n_row = lax.axis_size("row")
    n_col = lax.axis_size("col")
    row_index = lax.axis_index("row")
    col_index = lax.axis_index("col")
    group_rows = rows_col * n_col
    rows_row = group_rows // n_row
    per_col = rows_col // SEQ
    per_row = rows_row // SEQ
    group_first = lax.axis_index("dp") * (group_rows // SEQ)
    lengths_col = lax.dynamic_slice(lengths, (group_first + col_index * per_col,), (per_col,))
    lengths_row = lax.dynamic_slice(lengths, (group_first + row_index * per_row,), (per_row,))
    live = (
        (jnp.arange(SEQ)[None, :] < lengths_col[:, None]).astype(jnp.float32).reshape(rows_col, 1)
    )
    heads_local = width_col // HD
    orders = lax.dynamic_slice(block_order, (col_index * heads_local, 0), (heads_local, 2))
    row_start = row_index * width_row
    col_start = col_index * width_col
    ff_start = col_index * ff_col
    b_query_here = lax.dynamic_slice_in_dim(b_query, col_start, width_col)
    b_value_here = lax.dynamic_slice_in_dim(b_value, col_start, width_col)
    b_inter_here = lax.dynamic_slice_in_dim(b_inter, ff_start, ff_col)
    b_attn_here = lax.dynamic_slice_in_dim(b_attn_out, row_start, width_row)
    b_ffout_here = lax.dynamic_slice_in_dim(b_ffout, row_start, width_row)
    gain_one_here = lax.dynamic_slice_in_dim(gain_one, row_start, width_row)
    shift_one_here = lax.dynamic_slice_in_dim(shift_one, row_start, width_row)
    gain_two_here = lax.dynamic_slice_in_dim(gain_two, row_start, width_row)
    shift_two_here = lax.dynamic_slice_in_dim(shift_two, row_start, width_row)
    qkv_w = jnp.concatenate(
        [w_query.astype(jnp.bfloat16), w_key.astype(jnp.bfloat16), w_value.astype(jnp.bfloat16)], 1
    )
    attn_w = w_attn_out.astype(jnp.bfloat16)
    inter_w = w_inter.astype(jnp.bfloat16)
    ffout_w = w_ffout.astype(jnp.bfloat16)
    whole_tokens = gather_cols(tokens)
    qkv_total = sum_rows(product(whole_tokens, qkv_w))
    query_low = (qkv_total[:, :width_col] + b_query_here).astype(jnp.bfloat16)
    key_low = qkv_total[:, width_col : 2 * width_col].astype(jnp.bfloat16)
    value_low = (qkv_total[:, 2 * width_col :] + b_value_here).astype(jnp.bfloat16)
    blended_attention_output, logsum = attend_forward(
        query_low, key_low[None], value_low[None], orders, lengths_row, 2, 0, SEQ
    )
    whole_mixed = gather_rows(blended_attention_output.astype(jnp.bfloat16))
    residual_one = tokens.astype(jnp.float32) + sum_cols(product(whole_mixed, attn_w)) + b_attn_here
    normed_one, normal_one, scale_one = norm_forward(
        residual_one, gain_one_here, shift_one_here, shared_sums
    )
    whole_normed = gather_cols(normed_one.astype(jnp.bfloat16))
    hidden_pre = sum_rows(product(whole_normed, inter_w)) + b_inter_here
    hidden, gelu_back = jax.vjp(gelu_exact, hidden_pre)
    whole_hidden = gather_rows(hidden.astype(jnp.bfloat16))
    residual_two = normed_one + sum_cols(product(whole_hidden, ffout_w)) + b_ffout_here
    layer_out, normal_two, scale_two = norm_forward(
        residual_two, gain_two_here, shift_two_here, shared_sums
    )
    grad_out = cotangent.astype(jnp.float32) * live
    grad_gain_two = jnp.sum(grad_out * normal_two, 0)
    grad_shift_two = jnp.sum(grad_out, 0)
    grad_two = norm_backward(grad_out, normal_two, scale_two, gain_two_here, shared_sums)
    grad_b_ffout = jnp.sum(grad_two, 0)
    whole_grad_two = gather_cols(grad_two.astype(jnp.bfloat16))
    grad_hidden = sum_rows(transposed(whole_grad_two, ffout_w))
    grad_w_ffout = outer_sum(whole_hidden, whole_grad_two)
    (grad_pre,) = gelu_back(grad_hidden)
    grad_pre_low = grad_pre.astype(jnp.bfloat16)
    grad_b_inter = jnp.sum(grad_pre_low.astype(jnp.float32), 0)
    whole_grad_pre = gather_rows(grad_pre_low)
    grad_w_inter = outer_sum(whole_normed, whole_grad_pre)
    grad_normed = grad_two + sum_cols(transposed(whole_grad_pre, inter_w))
    grad_gain_one = jnp.sum(grad_normed * normal_one, 0)
    grad_shift_one = jnp.sum(grad_normed, 0)
    grad_one = norm_backward(grad_normed, normal_one, scale_one, gain_one_here, shared_sums)
    grad_b_attn_out = jnp.sum(grad_one, 0)
    whole_grad_one = gather_cols(grad_one.astype(jnp.bfloat16))
    grad_mixed = sum_rows(transposed(whole_grad_one, attn_w))
    grad_w_attn_out = outer_sum(whole_mixed, whole_grad_one)
    grad_query, grad_key, grad_value = attend_backward(
        query_low,
        key_low[None],
        value_low[None],
        grad_mixed.astype(jnp.bfloat16),
        logsum,
        orders,
        lengths_row,
        2,
        0,
        SEQ,
    )
    grad_qkv_low = jnp.concatenate(
        [
            grad_query.astype(jnp.bfloat16),
            grad_key[0].astype(jnp.bfloat16),
            grad_value[0].astype(jnp.bfloat16),
        ],
        1,
    )
    grad_b_query = jnp.sum(grad_qkv_low[:, :width_col].astype(jnp.float32), 0)
    grad_b_value = jnp.sum(grad_qkv_low[:, 2 * width_col :].astype(jnp.float32), 0)
    whole_grad_qkv = gather_rows(grad_qkv_low)
    grad_tokens = grad_one + sum_cols(transposed(whole_grad_qkv, qkv_w))
    grad_qkv_w = outer_sum(whole_tokens, whole_grad_qkv)
    weight_parts = (
        grad_qkv_w[:, :width_col],
        grad_qkv_w[:, width_col : 2 * width_col],
        grad_qkv_w[:, 2 * width_col :],
        grad_w_attn_out,
        grad_w_inter,
        grad_w_ffout,
    )
    vector_parts = (
        placed(grad_b_query, col_start, D),
        placed(grad_b_value, col_start, D),
        placed(grad_b_attn_out, row_start, D),
        placed(grad_b_inter, ff_start, FF),
        placed(grad_b_ffout, row_start, D),
        placed(grad_gain_one, row_start, D),
        placed(grad_shift_one, row_start, D),
        placed(grad_gain_two, row_start, D),
        placed(grad_shift_two, row_start, D),
    )
    return (layer_out.astype(jnp.bfloat16), grad_tokens, weight_parts, vector_parts)


def per_device(
    tokens,
    w_query,
    w_key,
    w_value,
    w_attn_out,
    w_inter,
    w_ffout,
    b_query,
    b_value,
    b_attn_out,
    b_inter,
    b_ffout,
    gain_one,
    shift_one,
    gain_two,
    shift_two,
    lengths,
    block_order,
    cotangent,
):
    weights = (w_query, w_key, w_value, w_attn_out, w_inter, w_ffout)
    vectors = (
        b_query,
        b_value,
        b_attn_out,
        b_inter,
        b_ffout,
        gain_one,
        shift_one,
        gain_two,
        shift_two,
    )
    results = grid_plan(tokens, weights, vectors, lengths, block_order, cotangent)
    layer_out, grad_tokens, weight_parts, vector_parts = results
    grad_w_query, grad_w_key, grad_w_value, grad_w_attn_out, grad_w_inter, grad_w_ffout = (
        lax.psum(weight_parts[0].astype(jnp.bfloat16), "dp").astype(jnp.float32),
        lax.psum(weight_parts[1].astype(jnp.bfloat16), "dp").astype(jnp.float32),
        lax.psum(weight_parts[2].astype(jnp.bfloat16), "dp").astype(jnp.float32),
        lax.psum(weight_parts[3].astype(jnp.bfloat16), "dp").astype(jnp.float32),
        lax.psum(weight_parts[4].astype(jnp.bfloat16), "dp").astype(jnp.float32),
        lax.psum(weight_parts[5].astype(jnp.bfloat16), "dp").astype(jnp.float32),
    )
    (
        grad_b_query,
        grad_b_value,
        grad_b_attn_out,
        grad_b_inter,
        grad_b_ffout,
        grad_gain_one,
        grad_shift_one,
        grad_gain_two,
        grad_shift_two,
    ) = lax.psum(
        (
            vector_parts[0],
            vector_parts[1],
            vector_parts[2],
            vector_parts[3],
            vector_parts[4],
            vector_parts[5],
            vector_parts[6],
            vector_parts[7],
            vector_parts[8],
        ),
        ("dp", "row", "col"),
    )
    return (
        layer_out,
        grad_tokens,
        grad_w_query,
        grad_w_key,
        grad_w_value,
        grad_w_attn_out,
        grad_w_inter,
        grad_w_ffout,
        grad_b_query,
        grad_b_value,
        grad_b_attn_out,
        grad_b_inter,
        grad_b_ffout,
        grad_gain_one,
        grad_shift_one,
        grad_gain_two,
        grad_shift_two,
    )


def solution(mesh):
    return jax.shard_map(
        per_device,
        mesh=mesh,
        in_specs=(
            P(("dp", "col"), "row"),
            P("row", "col"),
            P("row", "col"),
            P("row", "col"),
            P("col", "row"),
            P("row", "col"),
            P("col", "row"),
            P(),
            P(),
            P(),
            P(),
            P(),
            P(),
            P(),
            P(),
            P(),
            P(),
            P(),
            P(("dp", "col"), "row"),
        ),
        out_specs=(
            P(("dp", "col"), "row"),
            P(("dp", "col"), "row"),
            P("row", "col"),
            P("row", "col"),
            P("row", "col"),
            P("col", "row"),
            P("row", "col"),
            P("col", "row"),
            P(),
            P(),
            P(),
            P(),
            P(),
            P(),
            P(),
            P(),
            P(),
        ),
        check_vma=False,
    )
```

profile of v0, /device:TPU:0, one launch (start us, length us, event | category | flops | bytes accessed | tf_op | source)
XLA Modules:
  0.0 1184.7 jit_solution(4707898755306142605)
XLA Ops:
  10.4 46.9 %all-gather.9.cloned.1.call-done = bf16[4096,384]{1,0:T(8,128)(2,1)} async-done(((bf16[2048,384]{1,0:T(8,128)(2,1)}), bf16[4096,384]{1,0:T(8,128)(2,1)}) %all-gather.9.cloned.1.call-update) | async-done | bytes 3145744 | tf_op jit(solution)/shard_map/all_gather | solution.py:39
  57.3 10.9 convolution_bitcast_fusion.1
  69.7 27.0 %reduce-scatter.9.cloned.1.call-done = f32[2048,1152]{0,1:T(8,128)} async-done(((f32[4096,1152]{0,1:T(8,128)}), f32[2048,1152]{0,1:T(8,128)}) %reduce-scatter.9.cloned.1.call-update) | async-done | bytes 9437200 | tf_op jit(solution)/shard_map/reduce_scatter | solution.py:47
  108.7 84.4 %while.38 = (s32[]{:T(128)}, bf16[2048,384]{0,1:T(8,128)(2,1)}, f32[2048,6]{0,1:T(8,128)S(1)}, s32[6,2]{0,1:T(2,128)S(1)}, s32[1]{0:T(128)}, /*index=5*/bf16[204...) while((s32[]{:T(128)}, bf16[2048,384]{0,1:T(8,128)(2,1)}, ...), condition=%wide.region_4.5_spmd, body=%wide.region_1.4_spmd.sunk | while | flops 281019456 | bytes 13681410 | solution.py:133
  193.2 13.5 %all-gather.11.cloned.1.call-done = bf16[4096,384]{0,1:T(8,128)(2,1)} async-done(((bf16[2048,384]{0,1:T(8,128)(2,1)}), bf16[4096,384]{0,1:T(8,128)(2,1)}) %all-gather.11.cloned.1.call-update) | async-done | bytes 3145744 | tf_op jit(solution)/shard_map/all_gather | solution.py:43
  213.5 43.8 %reduce-scatter.11.cloned.1.call-done = bf16[2048,384]{1,0:T(8,128)(2,1)} async-done(((bf16[4096,384]{1,0:T(8,128)(2,1)}), bf16[2048,384]{1,0:T(8,128)(2,1)}) %reduce-scatter.11.cloned.1.call-update) | async-done | bytes 1572880 | tf_op jit(solution)/shard_map/reduce_scatter | solution.py:51
  265.2 44.9 %all-gather.13.cloned.1.call-done = bf16[4096,384]{1,0:T(8,128)(2,1)} async-done(((bf16[2048,384]{1,0:T(8,128)(2,1)}), bf16[4096,384]{1,0:T(8,128)(2,1)}) %all-gather.13.cloned.1.call-update) | async-done | bytes 3145744 | tf_op jit(solution)/shard_map/all_gather | solution.py:39
  310.1 13.8 %fusion.62 = f32[4096,1536]{1,0:T(8,128)} fusion(bf16[4096,384]{1,0:T(8,128)(2,1)} %all-gather.13.cloned.1.call-done, f32[384,1536]{1,0:T(8,128)} %param.28), kind=kOutput, calls=%fused_computation.116 | convolution fusion | flops 4832428032 | bytes 30670848 | tf_op jit(solution)/shard_map/dot_general | solution.py:15
  324.7 34.9 %reduce-scatter.13.cloned.1.call-done = f32[2048,1536]{1,0:T(8,128)} async-done(((f32[4096,1536]{1,0:T(8,128)}), f32[2048,1536]{1,0:T(8,128)}) %reduce-scatter.13.cloned.1.call-update) | async-done | bytes 12582928 | tf_op jit(solution)/shard_map/reduce_scatter | solution.py:47
  359.6 30.2 %multiply_convert_fusion.1 = (bf16[2048,1536]{1,0:T(8,128)(2,1)}, f32[2048,1536]{1,0:T(8,128)}) fusion(f32[2048,1536]{1,0:T(8,128)} %reduce-scatter.13.cloned.1.call-done, f32[1536]{0:T(1024)S(1)} %dynamic_slice.159), kind=kLoop, calls=%fused_computation.53 | loop fusion | flops 207618048 | bytes 31463424 | tf_op jit(solution)/shard_map/convert_element_type | solution.py:244
  389.8 26.2 %all-gather.15.cloned.1.call-done = bf16[4096,1536]{1,0:T(8,128)(2,1)} async-done(((bf16[2048,1536]{1,0:T(8,128)(2,1)}), bf16[4096,1536]{1,0:T(8,128)(2,1)}) %all-gather.15.cloned.1.call-update) | async-done | bytes 12582928 | tf_op jit(solution)/shard_map/all_gather | solution.py:43
  416.0 11.5 convolution_convert_fusion.3
  429.0 43.2 %reduce-scatter.15.cloned.1.call-done = bf16[2048,384]{1,0:T(8,128)(2,1)} async-done(((bf16[4096,384]{1,0:T(8,128)(2,1)}), bf16[2048,384]{1,0:T(8,128)(2,1)}) %reduce-scatter.15.cloned.1.call-update) | async-done | bytes 1572880 | tf_op jit(solution)/shard_map/reduce_scatter | solution.py:51
  487.0 6.4 fusion.73
  493.6 44.8 %all-gather.17.cloned.1.call-done = bf16[4096,384]{1,0:T(8,128)(2,1)} async-done(((bf16[2048,384]{1,0:T(8,128)(2,1)}), bf16[4096,384]{1,0:T(8,128)(2,1)}) %all-gather.17.cloned.1.call-update) | async-done | bytes 3145744 | tf_op jit(solution)/shard_map/all_gather | solution.py:39
  538.5 13.8 %fusion.58 = f32[4096,1536]{1,0:T(8,128)} fusion(bf16[4096,384]{1,0:T(8,128)(2,1)} %all-gather.17.cloned.1.call-done, f32[1536,384]{1,0:T(8,128)} %param.29), kind=kOutput, calls=%fused_computation.112 | convolution fusion | flops 4832428032 | bytes 30670848 | tf_op jit(solution)/shard_map/dot_general | solution.py:19
  552.4 35.5 %reduce-scatter.17.cloned.1.call-done = f32[2048,1536]{1,0:T(8,128)} async-done(((f32[4096,1536]{1,0:T(8,128)}), f32[2048,1536]{1,0:T(8,128)}) %reduce-scatter.17.cloned.1.call-update) | async-done | bytes 12582928 | tf_op jit(solution)/shard_map/reduce_scatter | solution.py:47
  587.9 17.0 %convert_reduce_fusion = (f32[1536]{0:T(1024)S(1)}, bf16[2048,1536]{1,0:T(8,128)(2,1)}) fusion(f32[2048,1536]{1,0:T(8,128)} %reduce-scatter.17.cloned.1.call-done, f32[2048,1536]{1,0:T(8,128)} %get-tuple-element.691, f32[2048,1536]{1,0:T(8,128)} %reduce-scatter.13.cloned.1.call-done, f32[1536]{0:T(1024)S(1)} %dynamic_slice.159), kind=kLoop, calls=%fused_computation.51 | loop fusion | flops 53475840 | bytes 44052480 | tf_op jit(solution)/shard_map/reduce_sum | solution.py:259
  605.0 26.2 %all-gather.19.cloned.1.call-done = bf16[4096,1536]{1,0:T(8,128)(2,1)} async-done(((bf16[2048,1536]{1,0:T(8,128)(2,1)}), bf16[4096,1536]{1,0:T(8,128)(2,1)}) %all-gather.19.cloned.1.call-update) | async-done | bytes 12582928 | tf_op jit(solution)/shard_map/all_gather | solution.py:43
  631.2 11.6 convolution_convert_fusion.2
  642.8 44.6 %reduce-scatter.19.cloned.1.call-done = bf16[2048,384]{1,0:T(8,128)(2,1)} async-done(((bf16[4096,384]{1,0:T(8,128)(2,1)}), bf16[2048,384]{1,0:T(8,128)(2,1)}) %reduce-scatter.19.cloned.1.call-update) | async-done | bytes 1572880 | tf_op jit(solution)/shard_map/reduce_scatter | solution.py:51
  701.8 44.8 %all-gather.21.cloned.1.call-done = bf16[4096,384]{1,0:T(8,128)(2,1)} async-done(((bf16[2048,384]{1,0:T(8,128)(2,1)}), bf16[4096,384]{1,0:T(8,128)(2,1)}) %all-gather.21.cloned.1.call-update) | async-done | bytes 3145744 | tf_op jit(solution)/shard_map/all_gather | solution.py:39
  746.6 6.6 fusion.64
  753.3 14.6 %reduce-scatter.21.cloned.1.call-done = f32[2048,384]{1,0:T(8,128)} async-done(((f32[4096,384]{1,0:T(8,128)}), f32[2048,384]{1,0:T(8,128)}) %reduce-scatter.21.cloned.1.call-update) | async-done | bytes 3145744 | tf_op jit(solution)/shard_map/reduce_scatter | solution.py:47
  772.8 175.0 %while.39 = (s32[]{:T(128)}, bf16[2048,384]{0,1:T(8,128)(2,1)S(1)}, bf16[1,2048,384]{1,2,0:T(8,128)(2,1)}, bf16[1,2048,384]{1,2,0:T(8,128)(2,1)S(1)}, s32[6,2]{0...) while((s32[]{:T(128)}, bf16[2048,384]{0,1:T(8,128)(2,1)S(1)}, ...), condition=%wide.region_29.30_spmd, body=%wide.region_27.29_spmd.sunk | while | flops 687866944 | bytes 34122520 | solution.py:183
  952.1 11.6 convolution_convert_fusion.4
  963.7 10.6 convolution_convert_fusion.5
  976.8 8.5 fusion.54
  986.6 9.3 convolution_convert_fusion.1
  999.2 45.3 %all-reduce = (f32[768]{0:T(1024)}, f32[768]{0:T(1024)}, f32[768]{0:T(1024)}, f32[3072]{0:T(1024)}, f32[768]{0:T(1024)}, /*index=5*/f32[768]{0:T(1024)}, f32[768]{0:T(1024)}, f32[768]{0:T(1024)}, f32[768]{0:T(1024)}) all-reduce(f32[768]{0:T(1024)S(1)} %dynamic_update_slice.82, ...), channel_id=1, replica_groups=mesh['dp'=8,'row'=2,'col'=2] {'dp','row','col'}, use_global_device_ids=true, to_apply=%region_38.39 | all-reduce | flops 9216 | bytes 73728 | tf_op jit(solution)/shard_map/psum | solution.py:370
  1044.5 85.6 %all-reduce.8.cloned.1.call-done = (bf16[384,384]{0,1:T(8,128)(2,1)}, bf16[384,384]{0,1:T(8,128)(2,1)}, bf16[384,384]{0,1:T(8,128)(2,1)}, bf16[384,384]{1,0:T(8,...) async-done(((bf16[384,384]{0,1:T(8,128)(2,1)}, bf16[384,384]{0,1:T(8,128)(2,1)}, bf16[384,384]{0,1:T(8,128)(2,1)}, bf16[384,384]{1,0:T(8,128)(2,1)}, ...) | async-done | bytes 3538960 | tf_op jit(solution)/shard_map/psum | solution.py:353
  1143.9 30.6 %reduce-scatter.23.cloned.1.call-done = bf16[2048,384]{1,0:T(8,128)(2,1)} async-done(((bf16[4096,384]{1,0:T(8,128)(2,1)}), bf16[2048,384]{1,0:T(8,128)(2,1)}) %reduce-scatter.23.cloned.1.call-update) | async-done | bytes 1572880 | tf_op jit(solution)/shard_map/reduce_scatter | solution.py:51
  (358 shorter events, 337.5 us)
Async XLA Ops:
  7.2 62.4 %copy-start = (s32[12,2]{0,1:T(2,128)S(1)}, s32[12,2]{0,1:T(2,128)}, u32[]{:S(2)}) copy-start(s32[12,2]{0,1:T(2,128)} %param.40) | copy-start | bytes 292
  7.2 3.1 copy-start.15
  7.2 50.0 %all-gather.9.cloned.1.call-start = ((), (), s32[]{:S(2)}) async-start(), calls=%async_computation.8 | async-start | bytes 4718592 | tf_op jit(solution)/shard_map/all_gather | solution.py:39
  8.0 88.7 %reduce-scatter.9.cloned.1.call-start = ((), (), s32[]{:S(2)}) async-start(), calls=%async_computation.9 | async-start | bytes 28311552 | tf_op jit(solution)/shard_map/reduce_scatter | solution.py:47
  9.1 59.0 %copy-start.10 = (bf16[384,384]{1,0:T(8,128)(2,1)}, bf16[384,384]{1,0:T(8,128)(2,1)S(1)}, u32[]{:S(2)}) copy-start(bf16[384,384]{1,0:T(8,128)(2,1)S(1)} %convert_element_type.176) | copy-start | bytes 884740
  10.3 57.8 %copy-start.12 = (bf16[384,384]{1,0:T(8,128)(2,1)}, bf16[384,384]{1,0:T(8,128)(2,1)S(1)}, u32[]{:S(2)}) copy-start(bf16[384,384]{1,0:T(8,128)(2,1)S(1)} %convert_element_type.177) | copy-start | bytes 884740
  10.4 57.8 %copy-start.13 = (bf16[384,384]{1,0:T(8,128)(2,1)}, bf16[384,384]{1,0:T(8,128)(2,1)S(1)}, u32[]{:S(2)}) copy-start(bf16[384,384]{1,0:T(8,128)(2,1)S(1)} %convert_element_type.178) | copy-start | bytes 884740
  68.2 138.6 %all-gather.11.cloned.1.call-start = ((), (), s32[]{:S(2)}) async-start(), calls=%async_computation.10 | async-start | bytes 4718592 | tf_op jit(solution)/shard_map/all_gather | solution.py:43
  193.1 13.6 %copy-start.6 = (bf16[1,2048,384]{2,1,0:T(8,128)(2,1)}, bf16[1,2048,384]{2,1,0:T(8,128)(2,1)S(1)}, u32[]{:S(2)}) copy-start(bf16[1,2048,384]{2,1,0:T(8,128)(2,1)S(1)} %get-tuple-element.1001) | copy-start | bytes 4718596
  193.2 19.4 %copy-start.7 = (bf16[2048,384]{1,0:T(8,128)(2,1)}, bf16[2048,384]{1,0:T(8,128)(2,1)S(1)}, u32[]{:S(2)}) copy-start(bf16[2048,384]{1,0:T(8,128)(2,1)S(1)} %get-tuple-element.1002) | copy-start | bytes 4718596
  193.2 64.2 %reduce-scatter.11.cloned.1.call-start = ((), (), s32[]{:S(2)}) async-start(), calls=%async_computation.11 | async-start | bytes 4718592 | tf_op jit(solution)/shard_map/reduce_scatter | solution.py:51
  212.6 44.7 %copy-start.2 = (bf16[2048,384]{1,0:T(8,128)(2,1)S(1)}, bf16[2048,384]{1,0:T(8,128)(2,1)}, u32[]{:S(2)}) copy-start(bf16[2048,384]{1,0:T(8,128)(2,1)} %param.23) | copy-start | bytes 4718596
  212.7 97.5 %all-gather.13.cloned.1.call-start = ((), (), s32[]{:S(2)}) async-start(), calls=%async_computation.12 | async-start | bytes 4718592 | tf_op jit(solution)/shard_map/all_gather | solution.py:39
  257.4 5.8 copy-start.3
  265.0 94.6 %reduce-scatter.13.cloned.1.call-start = ((), (), s32[]{:S(2)}) async-start(), calls=%async_computation.13 | async-start | bytes 37748736 | tf_op jit(solution)/shard_map/reduce_scatter | solution.py:47
  323.9 92.0 %all-gather.15.cloned.1.call-start = ((), (), s32[]{:S(2)}) async-start(), calls=%async_computation.14 | async-start | bytes 18874368 | tf_op jit(solution)/shard_map/all_gather | solution.py:43
  389.8 82.4 %reduce-scatter.15.cloned.1.call-start = ((), (), s32[]{:S(2)}) async-start(), calls=%async_computation.15 | async-start | bytes 4718592 | tf_op jit(solution)/shard_map/reduce_scatter | solution.py:51
  427.5 111.0 %all-gather.17.cloned.1.call-start = ((), (), s32[]{:S(2)}) async-start(), calls=%async_computation.16 | async-start | bytes 4718592 | tf_op jit(solution)/shard_map/all_gather | solution.py:39
  493.4 94.6 %reduce-scatter.17.cloned.1.call-start = ((), (), s32[]{:S(2)}) async-start(), calls=%async_computation.17 | async-start | bytes 37748736 | tf_op jit(solution)/shard_map/reduce_scatter | solution.py:47
  552.3 78.8 %all-gather.19.cloned.1.call-start = ((), (), s32[]{:S(2)}) async-start(), calls=%async_computation.18 | async-start | bytes 18874368 | tf_op jit(solution)/shard_map/all_gather | solution.py:43
  604.9 82.5 %reduce-scatter.19.cloned.1.call-start = ((), (), s32[]{:S(2)}) async-start(), calls=%async_computation.19 | async-start | bytes 4718592 | tf_op jit(solution)/shard_map/reduce_scatter | solution.py:51
  642.8 103.9 %all-gather.21.cloned.1.call-start = ((), (), s32[]{:S(2)}) async-start(), calls=%async_computation.20 | async-start | bytes 4718592 | tf_op jit(solution)/shard_map/all_gather | solution.py:39
  700.2 46.4 %copy-start.14 = (f32[384,384]{1,0:T(8,128)S(1)}, f32[384,384]{1,0:T(8,128)}, u32[]{:S(2)}) copy-start(f32[384,384]{1,0:T(8,128)} %param.27) | copy-start | bytes 1769476
  701.5 66.3 %reduce-scatter.21.cloned.1.call-start = ((), (), s32[]{:S(2)}) async-start(), calls=%async_computation.21 | async-start | bytes 9437184 | tf_op jit(solution)/shard_map/reduce_scatter | solution.py:47
  753.2 223.6 %all-gather.23.cloned.1.call-start = ((), (), s32[]{:S(2)}) async-start(), calls=%async_computation.22 | async-start | bytes 14155776 | tf_op jit(solution)/shard_map/all_gather | solution.py:43
  951.6 178.6 %all-reduce.8.cloned.1.call-start = ((), (), s32[]{:S(2)}) async-start(), calls=%async_computation.24 | async-start | bytes 7077888 | tf_op jit(solution)/shard_map/psum | solution.py:353
  952.1 11.6 copy-start.8
  963.7 10.6 copy-start.9
  963.7 10.6 copy-start.28
  986.4 188.2 %reduce-scatter.23.cloned.1.call-start = ((), (), s32[]{:S(2)}) async-start(), calls=%async_computation.23 | async-start | bytes 4718592 | tf_op jit(solution)/shard_map/reduce_scatter | solution.py:51
  1137.8 36.7 %copy-start.5 = (f32[2048,384]{1,0:T(8,128)S(1)}, f32[2048,384]{1,0:T(8,128)}, u32[]{:S(2)}) copy-start(f32[2048,384]{1,0:T(8,128)} %copy-done.4) | copy-start | bytes 9437188
  1141.1 36.9 %copy-start.1 = (s32[12,2]{0,1:T(2,128)S(1)}, s32[12,2]{0,1:T(2,128)}, u32[]{:S(2)}) copy-start(s32[12,2]{0,1:T(2,128)} %param.40) | copy-start | bytes 292
  (14 other events, 12.0 us)
Sparse Core Ops, SparseCore 0:
  9.6 47.6 all-gather.8
  68.3 28.2 reduce-scatter.8
  193.3 13.4 all-gather.10
  212.8 44.5 reduce-scatter.10
  265.1 44.9 all-gather.12
  324.1 35.4 reduce-scatter.12
  389.9 26.0 all-gather.14
  427.6 44.5 reduce-scatter.14
  493.5 44.9 all-gather.16
  552.5 35.4 reduce-scatter.16
  605.1 26.0 all-gather.18
  642.9 44.5 reduce-scatter.18
  701.7 44.9 all-gather.20
  753.3 14.4 reduce-scatter.20
  951.7 23.0 all-gather.22
  986.5 143.6 all-reduce.7
  1132.3 42.1 reduce-scatter.22
where the time goes:
time: 1200 us; the launch traced here: 1180 us
  waiting for transfers between devices  608 us (51%)
  matrix products  291 us (24%)
  other arithmetic  148 us (12%)
  blocking collectives  58.6 us (5%)
  local copies, waits for them, and re-layouts  43.4 us (4%)
  loops' own time  18.5 us (2%)
  between operations  14.5 us (1%)
    all_gather x4, waiting for transfers between devices, gather_cols(): return lax.all_gather(values, 'col', axis=0, tiled=True)  181 us
    reduce_scatter x4, waiting for transfers between devices, sum_cols(): lax.psum_scatter(values.astype(jnp.bfloat16), 'col', scatter_dimension=0,...  162 us
    reduce_scatter x4, waiting for transfers between devices, sum_rows(): return lax.psum_scatter(values, 'row', scatter_dimension=0, tiled=True)  112 us
    dot_general x40, matrix products, transposed(): lax.dot_general(left, right, (((1,), (1,)), ((), ())), preferred_element_...  106 us
    dot_general x28, matrix products, product(): return jnp.dot(left, right, preferred_element_type=jnp.float32)  96.1 us
    dot_general x28, matrix products, outer_sum(): lax.dot_general(left, right, (((0,), (0,)), ((), ())), preferred_element_...  88.9 us
    psum x1, waiting for transfers between devices, per_device(): lax.psum(weight_parts[0].astype(jnp.bfloat16), 'dp').astype(jnp.float32)  85.6 us
    all_gather x4, waiting for transfers between devices, gather_rows(): return lax.all_gather(values, 'row', axis=0, tiled=True)  65.9 us
  transfers between devices with their start and end apart: 17, of which 16 were waited for; matrix products, arithmetic and copies ran while one was open for 5% of the time, Pallas kernels for 0%

commit v1 on v0

--- a/solution.py
+++ b/solution.py
@@ -350,7 +350,9 @@
     results = grid_plan(tokens, weights, vectors, lengths, block_order, cotangent)
     layer_out, grad_tokens, weight_parts, vector_parts = results
     grad_w_query, grad_w_key, grad_w_value, grad_w_attn_out, grad_w_inter, grad_w_ffout = (
-        lax.psum(weight_parts[0].astype(jnp.bfloat16), "dp").astype(jnp.float32),
+        jnp.sum(lax.all_gather(weight_parts[0].astype(jnp.bfloat16), "dp"), axis=0).astype(
+            jnp.float32
+        ),
         lax.psum(weight_parts[1].astype(jnp.bfloat16), "dp").astype(jnp.float32),
         lax.psum(weight_parts[2].astype(jnp.bfloat16), "dp").astype(jnp.float32),
         lax.psum(weight_parts[3].astype(jnp.bfloat16), "dp").astype(jnp.float32),

time: 1200 us -> 1240 us (1.033)
  waiting for transfers between devices: 608 us -> 654 us
    all_gather x0 -> x1, waiting for transfers between devices: none -> 45.4 us  [per_device(): lax.all_gather(weight_parts[0].astype(jnp.bfloat16), 'dp')]
  transfers between devices with their start and end apart: 17 -> 18, of which waited for: 16 -> 17; matrix products, arithmetic and copies ran while one was open for 5% -> 4% of each run, Pallas kernels for 0% -> 0%
where the time goes in v1:
time: 1240 us; the launch traced here: 1230 us
  waiting for transfers between devices  654 us (53%)
  matrix products  291 us (23%)
  other arithmetic  147 us (12%)
  blocking collectives  57.8 us (5%)
  local copies, waits for them, and re-layouts  44.9 us (4%)
  loops' own time  18.5 us (1%)
  between operations  15.1 us (1%)
    all_gather x4, waiting for transfers between devices, gather_cols(): return lax.all_gather(values, 'col', axis=0, tiled=True)  181 us
    reduce_scatter x4, waiting for transfers between devices, sum_cols(): lax.psum_scatter(values.astype(jnp.bfloat16), 'col', scatter_dimension=0,...  170 us
    reduce_scatter x4, waiting for transfers between devices, sum_rows(): return lax.psum_scatter(values, 'row', scatter_dimension=0, tiled=True)  112 us
    dot_general x40, matrix products, transposed(): lax.dot_general(left, right, (((1,), (1,)), ((), ())), preferred_element_...  106 us
    dot_general x28, matrix products, product(): return jnp.dot(left, right, preferred_element_type=jnp.float32)  96.1 us
    dot_general x28, matrix products, outer_sum(): lax.dot_general(left, right, (((0,), (0,)), ((), ())), preferred_element_...  88.8 us
    psum x1, waiting for transfers between devices, per_device(): lax.psum(weight_parts[1].astype(jnp.bfloat16), 'dp').astype(jnp.float32)  78.1 us
    all_gather x4, waiting for transfers between devices, gather_rows(): return lax.all_gather(values, 'row', axis=0, tiled=True)  65.8 us
  transfers between devices with their start and end apart: 18, of which 17 were waited for; matrix products, arithmetic and copies ran while one was open for 4% of the time, Pallas kernels for 0%

profile of v1, /device:TPU:0, one launch (start us, length us, event | category | flops | bytes accessed | tf_op | source)
XLA Modules:
  0.0 1231.1 jit_solution(8092135030662211717)
XLA Ops:
  10.4 46.9 %all-gather.11.cloned.1.call-done = bf16[4096,384]{1,0:T(8,128)(2,1)} async-done(((bf16[2048,384]{1,0:T(8,128)(2,1)}), bf16[4096,384]{1,0:T(8,128)(2,1)}) %all-gather.11.cloned.1.call-update) | async-done | bytes 3145744 | tf_op jit(solution)/shard_map/all_gather | solution.py:39
  57.3 10.9 convolution_bitcast_fusion.1
  69.7 27.0 %reduce-scatter.9.cloned.1.call-done = f32[2048,1152]{0,1:T(8,128)} async-done(((f32[4096,1152]{0,1:T(8,128)}), f32[2048,1152]{0,1:T(8,128)}) %reduce-scatter.9.cloned.1.call-update) | async-done | bytes 9437200 | tf_op jit(solution)/shard_map/reduce_scatter | solution.py:47
  108.8 84.4 %while.38 = (s32[]{:T(128)}, bf16[2048,384]{0,1:T(8,128)(2,1)}, f32[2048,6]{0,1:T(8,128)S(1)}, s32[6,2]{0,1:T(2,128)S(1)}, s32[1]{0:T(128)}, /*index=5*/bf16[204...) while((s32[]{:T(128)}, bf16[2048,384]{0,1:T(8,128)(2,1)}, ...), condition=%wide.region_4.5_spmd, body=%wide.region_1.4_spmd.sunk | while | flops 281019456 | bytes 13681410 | solution.py:133
  193.3 13.5 %all-gather.13.cloned.1.call-done = bf16[4096,384]{0,1:T(8,128)(2,1)} async-done(((bf16[2048,384]{0,1:T(8,128)(2,1)}), bf16[4096,384]{0,1:T(8,128)(2,1)}) %all-gather.13.cloned.1.call-update) | async-done | bytes 3145744 | tf_op jit(solution)/shard_map/all_gather | solution.py:43
  213.5 43.8 %reduce-scatter.11.cloned.1.call-done = bf16[2048,384]{1,0:T(8,128)(2,1)} async-done(((bf16[4096,384]{1,0:T(8,128)(2,1)}), bf16[2048,384]{1,0:T(8,128)(2,1)}) %reduce-scatter.11.cloned.1.call-update) | async-done | bytes 1572880 | tf_op jit(solution)/shard_map/reduce_scatter | solution.py:51
  265.3 44.8 %all-gather.15.cloned.1.call-done = bf16[4096,384]{1,0:T(8,128)(2,1)} async-done(((bf16[2048,384]{1,0:T(8,128)(2,1)}), bf16[4096,384]{1,0:T(8,128)(2,1)}) %all-gather.15.cloned.1.call-update) | async-done | bytes 3145744 | tf_op jit(solution)/shard_map/all_gather | solution.py:39
  310.1 13.8 %fusion.62 = f32[4096,1536]{1,0:T(8,128)} fusion(bf16[4096,384]{1,0:T(8,128)(2,1)} %all-gather.15.cloned.1.call-done, f32[384,1536]{1,0:T(8,128)} %param.28), kind=kOutput, calls=%fused_computation.117 | convolution fusion | flops 4832428032 | bytes 30670848 | tf_op jit(solution)/shard_map/dot_general | solution.py:15
  324.7 34.9 %reduce-scatter.13.cloned.1.call-done = f32[2048,1536]{1,0:T(8,128)} async-done(((f32[4096,1536]{1,0:T(8,128)}), f32[2048,1536]{1,0:T(8,128)}) %reduce-scatter.13.cloned.1.call-update) | async-done | bytes 12582928 | tf_op jit(solution)/shard_map/reduce_scatter | solution.py:47
  359.6 30.2 %multiply_convert_fusion.1 = (bf16[2048,1536]{1,0:T(8,128)(2,1)}, f32[2048,1536]{1,0:T(8,128)}) fusion(f32[2048,1536]{1,0:T(8,128)} %reduce-scatter.13.cloned.1.call-done, f32[1536]{0:T(1024)S(1)} %dynamic_slice.159), kind=kLoop, calls=%fused_computation.53 | loop fusion | flops 207618048 | bytes 31463424 | tf_op jit(solution)/shard_map/convert_element_type | solution.py:244
  389.8 26.2 %all-gather.17.cloned.1.call-done = bf16[4096,1536]{1,0:T(8,128)(2,1)} async-done(((bf16[2048,1536]{1,0:T(8,128)(2,1)}), bf16[4096,1536]{1,0:T(8,128)(2,1)}) %all-gather.17.cloned.1.call-update) | async-done | bytes 12582928 | tf_op jit(solution)/shard_map/all_gather | solution.py:43
  416.0 11.5 convolution_convert_fusion.3
  429.1 43.2 %reduce-scatter.15.cloned.1.call-done = bf16[2048,384]{1,0:T(8,128)(2,1)} async-done(((bf16[4096,384]{1,0:T(8,128)(2,1)}), bf16[2048,384]{1,0:T(8,128)(2,1)}) %reduce-scatter.15.cloned.1.call-update) | async-done | bytes 1572880 | tf_op jit(solution)/shard_map/reduce_scatter | solution.py:51
  493.9 44.6 %all-gather.19.cloned.1.call-done = bf16[4096,384]{1,0:T(8,128)(2,1)} async-done(((bf16[2048,384]{1,0:T(8,128)(2,1)}), bf16[4096,384]{1,0:T(8,128)(2,1)}) %all-gather.19.cloned.1.call-update) | async-done | bytes 3145744 | tf_op jit(solution)/shard_map/all_gather | solution.py:39
  538.5 13.8 %fusion.58 = f32[4096,1536]{1,0:T(8,128)} fusion(bf16[4096,384]{1,0:T(8,128)(2,1)} %all-gather.19.cloned.1.call-done, f32[1536,384]{1,0:T(8,128)} %param.29), kind=kOutput, calls=%fused_computation.113 | convolution fusion | flops 4832428032 | bytes 30670848 | tf_op jit(solution)/shard_map/dot_general | solution.py:19
  552.4 35.5 %reduce-scatter.17.cloned.1.call-done = f32[2048,1536]{1,0:T(8,128)} async-done(((f32[4096,1536]{1,0:T(8,128)}), f32[2048,1536]{1,0:T(8,128)}) %reduce-scatter.17.cloned.1.call-update) | async-done | bytes 12582928 | tf_op jit(solution)/shard_map/reduce_scatter | solution.py:47
  588.0 17.0 %convert_reduce_fusion = (f32[1536]{0:T(1024)S(1)}, bf16[2048,1536]{1,0:T(8,128)(2,1)}) fusion(f32[2048,1536]{1,0:T(8,128)} %reduce-scatter.17.cloned.1.call-done, f32[2048,1536]{1,0:T(8,128)} %get-tuple-element.726, f32[2048,1536]{1,0:T(8,128)} %reduce-scatter.13.cloned.1.call-done, f32[1536]{0:T(1024)S(1)} %dynamic_slice.159), kind=kLoop, calls=%fused_computation.51 | loop fusion | flops 53475840 | bytes 44052480 | tf_op jit(solution)/shard_map/reduce_sum | solution.py:259
  605.0 26.2 %all-gather.21.cloned.1.call-done = bf16[4096,1536]{1,0:T(8,128)(2,1)} async-done(((bf16[2048,1536]{1,0:T(8,128)(2,1)}), bf16[4096,1536]{1,0:T(8,128)(2,1)}) %all-gather.21.cloned.1.call-update) | async-done | bytes 12582928 | tf_op jit(solution)/shard_map/all_gather | solution.py:43
  631.2 11.6 convolution_convert_fusion.2
  642.9 44.6 %reduce-scatter.19.cloned.1.call-done = bf16[2048,384]{1,0:T(8,128)(2,1)} async-done(((bf16[4096,384]{1,0:T(8,128)(2,1)}), bf16[2048,384]{1,0:T(8,128)(2,1)}) %reduce-scatter.19.cloned.1.call-update) | async-done | bytes 1572880 | tf_op jit(solution)/shard_map/reduce_scatter | solution.py:51
  701.8 44.9 %all-gather.23.cloned.1.call-done = bf16[4096,384]{1,0:T(8,128)(2,1)} async-done(((bf16[2048,384]{1,0:T(8,128)(2,1)}), bf16[4096,384]{1,0:T(8,128)(2,1)}) %all-gather.23.cloned.1.call-update) | async-done | bytes 3145744 | tf_op jit(solution)/shard_map/all_gather | solution.py:39
  746.7 6.6 fusion.64
  753.4 14.6 %reduce-scatter.21.cloned.1.call-done = f32[2048,384]{1,0:T(8,128)} async-done(((f32[4096,384]{1,0:T(8,128)}), f32[2048,384]{1,0:T(8,128)}) %reduce-scatter.21.cloned.1.call-update) | async-done | bytes 3145744 | tf_op jit(solution)/shard_map/reduce_scatter | solution.py:47
  772.9 175.0 %while.39 = (s32[]{:T(128)}, bf16[2048,384]{0,1:T(8,128)(2,1)S(1)}, bf16[1,2048,384]{1,2,0:T(8,128)(2,1)}, bf16[1,2048,384]{1,2,0:T(8,128)(2,1)S(1)}, s32[6,2]{0...) while((s32[]{:T(128)}, bf16[2048,384]{0,1:T(8,128)(2,1)S(1)}, ...), condition=%wide.region_29.30_spmd, body=%wide.region_27.29_spmd.sunk | while | flops 687866944 | bytes 34122520 | solution.py:183
  951.9 11.6 convolution_convert_fusion.4
  963.5 10.5 convolution_convert_fusion.5
  976.5 8.5 fusion.54
  987.0 9.3 convolution_convert_fusion.1
  999.6 44.5 %all-reduce = (f32[768]{0:T(1024)}, f32[768]{0:T(1024)}, f32[768]{0:T(1024)}, f32[3072]{0:T(1024)}, f32[768]{0:T(1024)}, /*index=5*/f32[768]{0:T(1024)}, f32[768]{0:T(1024)}, f32[768]{0:T(1024)}, f32[768]{0:T(1024)}) all-reduce(f32[768]{0:T(1024)S(1)} %dynamic_update_slice.82, ...), channel_id=1, replica_groups=mesh['dp'=8,'row'=2,'col'=2] {'dp','row','col'}, use_global_device_ids=true, to_apply=%region_38.39 | all-reduce | flops 9216 | bytes 73728 | tf_op jit(solution)/shard_map/psum | solution.py:372
  1044.1 78.1 %all-reduce.8.cloned.1.call-done = (bf16[384,384]{0,1:T(8,128)(2,1)}, bf16[384,384]{0,1:T(8,128)(2,1)}, bf16[384,384]{1,0:T(8,128)(2,1)}, bf16[384,1536]{1,0:T(8,128)(2,1)}, bf16[1536,384]{1,0:T(8,128)(2,1)}) async-done(((bf16[384,384]{0,1:T(8,128)(2,1)}, bf16[384,384]{0,1:T(8,128)(2,1)}, bf16[384,384]{1,0:T(8,128)(2,1)}, bf16[384,1536]{1,0:T(8,128)(2,1)}, bf16[1536,384]{1,0:T(8,128)(2,1)}), ...) | async-done | bytes 3244048 | tf_op jit(solution)/shard_map/psum | solution.py:356
  1131.3 45.4 %all-gather.27.cloned.1.call-done = bf16[3072,384]{0,1:T(8,128)(2,1)} async-done(((bf16[384,384]{0,1:T(8,128)(2,1)}), bf16[3072,384]{0,1:T(8,128)(2,1)}) %all-gather.27.cloned.1.call-update) | async-done | bytes 2359312 | tf_op jit(solution)/shard_map/all_gather | solution.py:353
  1181.9 38.5 %reduce-scatter.23.cloned.1.call-done = bf16[2048,384]{1,0:T(8,128)(2,1)} async-done(((bf16[4096,384]{1,0:T(8,128)(2,1)}), bf16[2048,384]{1,0:T(8,128)(2,1)}) %reduce-scatter.23.cloned.1.call-update) | async-done | bytes 1572880 | tf_op jit(solution)/shard_map/reduce_scatter | solution.py:51
  (367 shorter events, 344.8 us)
Async XLA Ops:
  7.2 62.4 %copy-start = (s32[12,2]{0,1:T(2,128)S(1)}, s32[12,2]{0,1:T(2,128)}, u32[]{:S(2)}) copy-start(s32[12,2]{0,1:T(2,128)} %param.40) | copy-start | bytes 292
  7.2 50.0 %all-gather.11.cloned.1.call-start = ((), (), s32[]{:S(2)}) async-start(), calls=%async_computation.8 | async-start | bytes 4718592 | tf_op jit(solution)/shard_map/all_gather | solution.py:39
  8.0 88.8 %reduce-scatter.9.cloned.1.call-start = ((), (), s32[]{:S(2)}) async-start(), calls=%async_computation.9 | async-start | bytes 28311552 | tf_op jit(solution)/shard_map/reduce_scatter | solution.py:47
  9.1 59.1 %copy-start.12 = (bf16[384,384]{1,0:T(8,128)(2,1)}, bf16[384,384]{1,0:T(8,128)(2,1)S(1)}, u32[]{:S(2)}) copy-start(bf16[384,384]{1,0:T(8,128)(2,1)S(1)} %convert_element_type.178) | copy-start | bytes 884740
  10.3 57.8 %copy-start.14 = (bf16[384,384]{1,0:T(8,128)(2,1)}, bf16[384,384]{1,0:T(8,128)(2,1)S(1)}, u32[]{:S(2)}) copy-start(bf16[384,384]{1,0:T(8,128)(2,1)S(1)} %convert_element_type.179) | copy-start | bytes 884740
  10.4 57.8 %copy-start.15 = (bf16[384,384]{1,0:T(8,128)(2,1)}, bf16[384,384]{1,0:T(8,128)(2,1)S(1)}, u32[]{:S(2)}) copy-start(bf16[384,384]{1,0:T(8,128)(2,1)S(1)} %convert_element_type.180) | copy-start | bytes 884740
  68.2 138.6 %all-gather.13.cloned.1.call-start = ((), (), s32[]{:S(2)}) async-start(), calls=%async_computation.10 | async-start | bytes 4718592 | tf_op jit(solution)/shard_map/all_gather | solution.py:43
  193.2 13.6 %copy-start.6 = (bf16[1,2048,384]{2,1,0:T(8,128)(2,1)}, bf16[1,2048,384]{2,1,0:T(8,128)(2,1)S(1)}, u32[]{:S(2)}) copy-start(bf16[1,2048,384]{2,1,0:T(8,128)(2,1)S(1)} %get-tuple-element.1035) | copy-start | bytes 4718596
  193.2 19.4 %copy-start.7 = (bf16[2048,384]{1,0:T(8,128)(2,1)}, bf16[2048,384]{1,0:T(8,128)(2,1)S(1)}, u32[]{:S(2)}) copy-start(bf16[2048,384]{1,0:T(8,128)(2,1)S(1)} %get-tuple-element.1036) | copy-start | bytes 4718596
  193.3 64.1 %reduce-scatter.11.cloned.1.call-start = ((), (), s32[]{:S(2)}) async-start(), calls=%async_computation.11 | async-start | bytes 4718592 | tf_op jit(solution)/shard_map/reduce_scatter | solution.py:51
  212.6 44.7 %copy-start.2 = (bf16[2048,384]{1,0:T(8,128)(2,1)S(1)}, bf16[2048,384]{1,0:T(8,128)(2,1)}, u32[]{:S(2)}) copy-start(bf16[2048,384]{1,0:T(8,128)(2,1)} %param.23) | copy-start | bytes 4718596
  212.7 97.5 %all-gather.15.cloned.1.call-start = ((), (), s32[]{:S(2)}) async-start(), calls=%async_computation.12 | async-start | bytes 4718592 | tf_op jit(solution)/shard_map/all_gather | solution.py:39
  265.0 94.6 %reduce-scatter.13.cloned.1.call-start = ((), (), s32[]{:S(2)}) async-start(), calls=%async_computation.13 | async-start | bytes 37748736 | tf_op jit(solution)/shard_map/reduce_scatter | solution.py:47
  324.0 92.0 %all-gather.17.cloned.1.call-start = ((), (), s32[]{:S(2)}) async-start(), calls=%async_computation.14 | async-start | bytes 18874368 | tf_op jit(solution)/shard_map/all_gather | solution.py:43
  389.8 82.4 %reduce-scatter.15.cloned.1.call-start = ((), (), s32[]{:S(2)}) async-start(), calls=%async_computation.15 | async-start | bytes 4718592 | tf_op jit(solution)/shard_map/reduce_scatter | solution.py:51
  427.5 111.0 %all-gather.19.cloned.1.call-start = ((), (), s32[]{:S(2)}) async-start(), calls=%async_computation.16 | async-start | bytes 4718592 | tf_op jit(solution)/shard_map/all_gather | solution.py:39
  493.4 94.6 %reduce-scatter.17.cloned.1.call-start = ((), (), s32[]{:S(2)}) async-start(), calls=%async_computation.17 | async-start | bytes 37748736 | tf_op jit(solution)/shard_map/reduce_scatter | solution.py:47
  552.4 78.8 %all-gather.21.cloned.1.call-start = ((), (), s32[]{:S(2)}) async-start(), calls=%async_computation.18 | async-start | bytes 18874368 | tf_op jit(solution)/shard_map/all_gather | solution.py:43
  605.0 82.5 %reduce-scatter.19.cloned.1.call-start = ((), (), s32[]{:S(2)}) async-start(), calls=%async_computation.19 | async-start | bytes 4718592 | tf_op jit(solution)/shard_map/reduce_scatter | solution.py:51
  642.8 103.9 %all-gather.23.cloned.1.call-start = ((), (), s32[]{:S(2)}) async-start(), calls=%async_computation.20 | async-start | bytes 4718592 | tf_op jit(solution)/shard_map/all_gather | solution.py:39
  700.3 46.4 %copy-start.16 = (f32[384,384]{1,0:T(8,128)S(1)}, f32[384,384]{1,0:T(8,128)}, u32[]{:S(2)}) copy-start(f32[384,384]{1,0:T(8,128)} %param.27) | copy-start | bytes 1769476
  701.6 66.4 %reduce-scatter.21.cloned.1.call-start = ((), (), s32[]{:S(2)}) async-start(), calls=%async_computation.21 | async-start | bytes 9437184 | tf_op jit(solution)/shard_map/reduce_scatter | solution.py:47
  753.3 223.2 %all-gather.25.cloned.1.call-start = ((), (), s32[]{:S(2)}) async-start(), calls=%async_computation.22 | async-start | bytes 14155776 | tf_op jit(solution)/shard_map/all_gather | solution.py:43
  951.6 170.6 %all-reduce.8.cloned.1.call-start = ((), (), s32[]{:S(2)}) async-start(), calls=%async_computation.25 | async-start | bytes 6488064 | tf_op jit(solution)/shard_map/psum | solution.py:356
  951.9 11.6 copy-start.8
  963.5 10.6 copy-start.9
  963.5 10.6 copy-start.30
  986.1 190.7 %all-gather.27.cloned.1.call-start = ((), (), s32[]{:S(2)}) async-start(), calls=%async_computation.24 | async-start | bytes 2654208 | tf_op jit(solution)/shard_map/all_gather | solution.py:353
  986.6 233.7 %reduce-scatter.23.cloned.1.call-start = ((), (), s32[]{:S(2)}) async-start(), calls=%async_computation.23 | async-start | bytes 4718592 | tf_op jit(solution)/shard_map/reduce_scatter | solution.py:51
  1122.2 7.6 copy-start.10
  1176.7 43.7 %copy-start.5 = (f32[2048,384]{1,0:T(8,128)S(1)}, f32[2048,384]{1,0:T(8,128)}, u32[]{:S(2)}) copy-start(f32[2048,384]{1,0:T(8,128)} %copy-done.4) | copy-start | bytes 9437188
  1180.9 42.9 %copy-start.1 = (s32[12,2]{0,1:T(2,128)S(1)}, s32[12,2]{0,1:T(2,128)}, u32[]{:S(2)}) copy-start(s32[12,2]{0,1:T(2,128)} %param.40) | copy-start | bytes 292
  (17 other events, 27.3 us)
Sparse Core Ops, SparseCore 0:
  9.6 47.6 all-gather.10
  68.3 28.3 reduce-scatter.8
  193.4 13.3 all-gather.12
  212.8 44.5 reduce-scatter.10
  265.1 44.9 all-gather.14
  324.1 35.4 reduce-scatter.12
  389.9 26.0 all-gather.16
  427.7 44.5 reduce-scatter.14
  493.5 44.9 all-gather.18
  552.5 35.4 reduce-scatter.16
  605.1 26.0 all-gather.20
  642.9 44.5 reduce-scatter.18
  701.7 44.9 all-gather.22
  753.4 14.4 reduce-scatter.20
  951.8 23.0 all-gather.24
  986.2 135.9 all-reduce.7
  1124.1 52.5 all-gather.26
  1178.8 41.5 reduce-scatter.22
